TPU v7x, 256 devices: a whole 4x4x8 slice. The times are simulated.
256 devices in a mesh: space: 32 (over x, y, core), mem: 8 (over z).
Axes of the slice: x: 4, y: 4, z: 8, core: 2. Of those that a mesh axis runs over, the one named last changes fastest.
Arguments:
- increment: float32 [16, 262144], P(None, 'space'), may hold values from -6 to 6
- anomalies: bfloat16 [64, 16, 262144], P('mem', None, 'space'), may hold values from -6 to 6
- interp_index: int32 [3, 262144], P(None, 'space'), may hold values from 0 to 2302, as said below
- interp_weight: float32 [3, 262144], P(None, 'space'), may hold values from 0.2 to 1
- neighbour_blocks: int32 [9, 512], P(None, 'space'), may hold values from 0 to 31, as said below
- tiles: bfloat16 [512, 9, 128, 128], P('space'), may hold values from -0.1875 to 0.1875
Outputs:
- covariance_image: float32 [16, 262144], P(None, ('space', 'mem'))
Inputs may be any that keep to these rules, and one draw needn't show every extreme that they name: `interp_index`: column j of a patch, at position i = j % 8192, names points from c - 128 to c + 127, where c = 128 + i * 2048 // 8192. `neighbour_blocks`: row 0 names the block itself (8 plus its place in the patch); the others lie within 8 blocks of it.
All inputs are finite; a program needn't handle non-finite values.
Results may differ from a plain program's by a relative error of at most 0.015.
Values may be sent and summed in bfloat16 or wider, within the bound.
A program may use at most 64 MiB of HBM per device.

v0:
```python
import jax
import jax.numpy as jnp
from jax import lax
from jax.sharding import PartitionSpec as P

BLOCK = 128
HI = 128
INTP = 3
SUB_DEV = 2048
HB = 8
HS = 1024


def with_halo(block, sides, width):
    for axis, dim in sides:
        count = lax.axis_size(axis)
        forward = [(i, i + 1) for i in range(count - 1)]
        backward = [(target, source) for source, target in forward]
        low = lax.ppermute(
            lax.slice_in_dim(block, block.shape[dim] - width, None, axis=dim), axis, forward
        )
        high = lax.ppermute(lax.slice_in_dim(block, 0, width, axis=dim), axis, backward)
        block = jnp.concatenate([low, block, high], axis=dim)
    return block


def in_blocks(array, dim, devices):
    before, after = (array.shape[:dim], array.shape[dim + 1 :])
    return jnp.moveaxis(array.reshape(*before, devices, -1, *after), dim, 0)


def summed_on_arrival(array, axis, dim):
    pieces = in_blocks(array, dim, lax.axis_size(axis))
    arrived = lax.all_to_all(pieces, axis, split_axis=0, concat_axis=0, tiled=True)
    return arrived.astype(jnp.float32).sum(axis=0)


def interp_table(interp_index, interp_weight, piece):
    columns = interp_index.shape[1]
    col_blocks = columns // (4 * piece)
    index_blocks = interp_index.reshape(INTP, col_blocks, 4 * piece)
    weight_blocks = interp_weight.reshape(INTP, col_blocks, 4 * piece)
    base = (jnp.arange(col_blocks, dtype=jnp.int32) * piece)[:, None]
    slots = jnp.arange(3 * piece, dtype=jnp.int32)
    table = jnp.zeros((col_blocks, 3 * piece, 4 * piece), jnp.float32)
    for which in range(INTP):
        local = index_blocks[which] - base
        table = table + jnp.where(
            local[:, None, :] == slots[None, :, None], weight_blocks[which][:, None, :], 0.0
        )
    return table


def shards(increment, anomalies, interp_index, interp_weight, neighbour_blocks, tiles):
    mem_dev, n_fields, columns = anomalies.shape
    row_count = mem_dev * n_fields
    piece = HI
    col_blocks = columns // (4 * piece)
    table = interp_table(interp_index, interp_weight, piece)
    weighted = (anomalies.astype(jnp.float32) * increment[None]).reshape(
        row_count, col_blocks, 4 * piece
    )
    window = jnp.einsum("rcj,cpj->rcp", weighted, table)
    window = window.reshape(row_count, col_blocks, 3, piece)
    spread = jnp.pad(window[:, :, 0], ((0, 0), (0, 2), (0, 0)))
    spread = spread + jnp.pad(window[:, :, 1], ((0, 0), (1, 1), (0, 0)))
    spread = spread + jnp.pad(window[:, :, 2], ((0, 0), (2, 0), (0, 0)))
    spread = spread.reshape(row_count, SUB_DEV + 2 * HI)
    reach = HS + HI
    padded = with_halo(spread.astype(jnp.bfloat16), (("space", 1),), reach).astype(spread.dtype)
    left_tail = padded[:, :reach]
    own_part = padded[:, reach : reach + SUB_DEV + 2 * HI]
    right_head = padded[:, reach + SUB_DEV + 2 * HI :]
    full_sum = jnp.zeros((row_count, SUB_DEV + 2 * HS), jnp.float32)
    full_sum = full_sum.at[:, :reach].add(left_tail)
    full_sum = full_sum.at[:, HS - HI : HS + SUB_DEV + HI].add(own_part)
    full_sum = full_sum.at[:, HS + SUB_DEV - HI :].add(right_head)
    device_index = lax.axis_index("space")
    dev_count = lax.axis_size("space")
    position = jnp.arange(SUB_DEV + 2 * HS, dtype=jnp.int32)
    outside = (position < HS) & (device_index == 0) | (position >= HS + SUB_DEV) & (
        device_index == dev_count - 1
    )
    full_sum = jnp.where(outside[None, :], 0.0, full_sum)
    sub_wide = full_sum.astype(jnp.bfloat16)
    ext_blocks = SUB_DEV // BLOCK + 2 * HB
    blocked = sub_wide.reshape(row_count, ext_blocks, BLOCK)
    selector = (
        neighbour_blocks[:, :, None] == jnp.arange(ext_blocks, dtype=jnp.int32)[None, None, :]
    ).astype(jnp.bfloat16)
    picked = jnp.einsum(
        "rek,nbe->rnbk", blocked, selector, preferred_element_type=jnp.float32
    ).astype(jnp.bfloat16)
    smooth = jnp.einsum("rnbk,bnkl->rbl", picked, tiles, preferred_element_type=jnp.float32)
    smooth = smooth.reshape(row_count, SUB_DEV).astype(jnp.bfloat16)
    smooth_wide = with_halo(smooth, (("space", 1),), HI)
    pieces = smooth_wide.astype(jnp.float32).reshape(row_count, col_blocks + 2, piece)
    windows = jnp.concatenate(
        [pieces[:, :col_blocks], pieces[:, 1 : col_blocks + 1], pieces[:, 2:]], axis=2
    )
    returned = jnp.einsum("rcp,cpj->rcj", windows, table)
    partial_value = jnp.sum(
        anomalies.astype(jnp.float32) * returned.reshape(mem_dev, n_fields, columns), axis=0
    )
    members = mem_dev * lax.axis_size("mem")
    summed = summed_on_arrival(partial_value.astype(jnp.bfloat16), "mem", 1)
    return summed / (members - 1)


def solution(mesh):
    in_specs = (
        P(None, "space"),
        P("mem", None, "space"),
        P(None, "space"),
        P(None, "space"),
        P(None, "space"),
        P("space", None, None, None),
    )
    out_specs = P(None, ("space", "mem"))
    return jax.shard_map(shards, mesh=mesh, in_specs=in_specs, out_specs=out_specs, check_vma=False)
```

profile of v0, /device:TPU:2, one launch (start us, length us, event | category | flops | bytes accessed | tf_op | source)
XLA Modules:
  0.0 97.8 jit_solution(12741716818037349832)
XLA Ops:
  0.0 1.3 %slice_reduce_fusion.5 = (s32[8192]{0:T(1024)S(1)}, s32[8192]{0:T(1024)S(1)}, s32[8192]{0:T(1024)S(1)}) fusion(s32[3,8192]{1,0:T(4,128)} %param.14), kind=kLoop, calls=%fused_computation.58 | loop fusion | bytes 196608 | tf_op jit(solution)/shard_map/slice | solution.py:47
  1.4 1.3 %slice_reduce_fusion.4 = (f32[8192]{0:T(1024)S(1)}, f32[8192]{0:T(1024)S(1)}, f32[8192]{0:T(1024)S(1)}) fusion(f32[3,8192]{1,0:T(4,128)} %param.15), kind=kLoop, calls=%fused_computation.57 | loop fusion | bytes 196608 | tf_op jit(solution)/shard_map/slice | solution.py:49
  2.7 2.1 %convert_multiply_fusion.1 = bf16[8,16,8192]{2,1,0:T(8,128)(2,1)S(1)} fusion(bf16[8,16,8192]{2,1,0:T(8,128)(2,1)} %param.13, f32[16,8192]{1,0:T(8,128)} %param.12), kind=kLoop, calls=%fused_computation.21 | loop fusion | flops 3145728 | bytes 4718592 | tf_op jit(solution)/shard_map/mul | solution.py:60
  4.8 0.9 copy.58
  5.7 0.1 broadcast_subtract_fusion.2
  5.8 14.1 %fusion.1 = f32[16,384,128]{2,1,0:T(8,128)S(1)} fusion(f32[16,512]{1,0:T(8,128)S(1)} %broadcast_in_dim.59, s32[16,512]{1,0:T(8,128)S(1)} %get-tuple-element.59, f32[16,512]{1,0:T(8,128)S(1)} %broadcast_in_dim.57, s32[16,512]{1,0:T(8,128)S(1)} %get-tuple-element.58, f32[16,512]{1,0:T(8,128)S(1)} %broadcast_in_dim.54, s32[16,512]{1,0:T(8,128)S(1)} %get-tuple-element.57, ...), kind=kOutput, calls=%fused_computation.5 | convolution fusion | flops 830472192 | bytes 5439488 | tf_op jit(solution)/shard_map/rcj,cpj->rcp/dot_general | solution.py:63
  19.9 0.3 slice_bitcast_fusion.2
  20.2 0.2 add_convert_fusion
  20.4 0.2 copy.39
  20.7 1.9 %collective-permute-start = (bf16[128,1152]{1,0:T(8,128)(2,1)S(1)}, bf16[128,1152]{1,0:T(8,128)(2,1)S(1)}, u32[]{:S(2)}, u32[]{:S(2)}) collective-permute-start(bf16[128,1152]{1,0:T(8,128)(2,1)S(1)} %get-tuple-element.53), channel_id=1, source_target_pairs={{0,8},{8,16},{16,24},{24,32},{32,40},{40,48},{48,56},{56,64},{64,7... | collective-permute-start | bytes 884744 | tf_op jit(solution)/shard_map/ppermute | solution.py:19
  22.7 5.8 %collective-permute-start.1 = (bf16[128,1152]{1,0:T(8,128)(2,1)S(1)}, bf16[128,1152]{1,0:T(8,128)(2,1)S(1)}, u32[]{:S(2)}, u32[]{:S(2)}) collective-permute-start(bf16[128,1152]{1,0:T(8,128)(2,1)S(1)} %get-tuple-element.54), channel_id=1, source_target_pairs={{8,0},{16,8},{24,16},{32,24},{40,32},{48,40},{56,48},{64,56},{72,6... | collective-permute-start | bytes 884744 | tf_op jit(solution)/shard_map/ppermute | solution.py:22
  28.4 0.6 compare_reduce_fusion.1
  29.1 0.7 compare_reduce_fusion
  29.8 1.1 %collective-permute-done = bf16[128,1152]{1,0:T(8,128)(2,1)S(1)} collective-permute-done((bf16[128,1152]{1,0:T(8,128)(2,1)S(1)}, bf16[128,1152]{1,0:T(8,128)(2,1)S(1)}, u32[]{:S(2)}, u32[]{:S(2)}) %collective-permute-start) | collective-permute-done | bytes 294944 | tf_op jit(solution)/shard_map/ppermute | solution.py:19
  30.9 1.8 %collective-permute-done.1 = bf16[128,1152]{1,0:T(8,128)(2,1)S(1)} collective-permute-done((bf16[128,1152]{1,0:T(8,128)(2,1)S(1)}, bf16[128,1152]{1,0:T(8,128)(2,1)S(1)}, u32[]{:S(2)}, u32[]{:S(2)}) %collective-permute-start.1) | collective-permute-done | bytes 294944 | tf_op jit(solution)/shard_map/ppermute | solution.py:22
  32.6 0.7 convert_select_fusion
  33.3 0.2 scatter-add.10
  33.6 0.2 maximum_convert_fusion
  33.8 1.2 %fusion.34 = f32[128,4096]{1,0:T(8,128)S(1)} fusion(f32[128,4096]{1,0:T(8,128)S(1)} %scatter-add.10, f32[128,4608]{1,0:T(8,128)S(1)} %maximum_convert_fusion, pred[]{:T(512)} %compare_reduce_fusion), kind=kLoop, calls=%fused_computation.37 | loop fusion | flops 589824 | bytes 3538945 | tf_op jit(solution)/shard_map/scatter-add | solution.py:76
  35.0 0.0 slice-start
  35.0 0.1 fusion.36
  35.1 0.0 copy-start.1
  35.1 0.2 fusion.35
  35.4 0.0 slice-start.1
  35.4 0.2 copy.59
  35.7 0.3 copy-done.1
  36.0 1.4 %convert_bitcast_fusion = bf16[128,9,16,128]{3,2,0,1:T(8,128)(2,1)S(1)} fusion(bf16[128,32,128,1]{2,1,0,3:T(8,128)(2,1)S(1)} %bitcast.52, s32[9,16]{1,0:T(8,128)S(1)} %copy-done.1), kind=kOutput, calls=%fused_computation.24 | convolution fusion | flops 153358848 | bytes 5767744 | tf_op jit(solution)/shard_map/rek,nbe->rnbk/dot_general | solution.py:91
  37.4 0.0 slice-done
  37.4 0.0 slice-done.1
  37.4 2.9 %fusion.31 = bf16[16,128,128]{1,2,0:T(8,128)(2,1)S(1)} fusion(bf16[16,9,128,128]{3,2,1,0:T(8,128)(2,1)S(1)} %bitcast.61, bf16[128,9,16,128]{3,2,0,1:T(8,128)(2,1)S(1)} %convert_bitcast_fusion), kind=kOutput, calls=%fused_computation.36 | convolution fusion | flops 604241920 | bytes 9961472 | tf_op jit(solution)/shard_map/rnbk,bnkl->rbl/dot_general | solution.py:94
  40.3 1.9 %collective-permute-start.2 = (bf16[128,128]{0,1:T(8,128)(2,1)S(1)}, bf16[128,128]{0,1:T(8,128)(2,1)S(1)}, u32[]{:S(2)}, u32[]{:S(2)}) collective-permute-start(bf16[128,128]{0,1:T(8,128)(2,1)S(1)} %get-tuple-element.55), channel_id=1, source_target_pairs={{0,8},{8,16},{16,24},{24,32},{32,40},{40,48},{48,56},{56,64},{64,7... | collective-permute-start | bytes 98312 | tf_op jit(solution)/shard_map/ppermute | solution.py:19
  42.2 6.1 %collective-permute-start.3 = (bf16[128,128]{0,1:T(8,128)(2,1)S(1)}, bf16[128,128]{0,1:T(8,128)(2,1)S(1)}, u32[]{:S(2)}, u32[]{:S(2)}) collective-permute-start(bf16[128,128]{0,1:T(8,128)(2,1)S(1)} %get-tuple-element.56), channel_id=1, source_target_pairs={{8,0},{16,8},{24,16},{32,24},{40,32},{48,40},{56,48},{64,56},{72,6... | collective-permute-start | bytes 98312 | tf_op jit(solution)/shard_map/ppermute | solution.py:22
  48.4 0.0 collective-permute-done.2
  48.4 1.4 %collective-permute-done.3 = bf16[128,128]{0,1:T(8,128)(2,1)S(1)} collective-permute-done((bf16[128,128]{0,1:T(8,128)(2,1)S(1)}, bf16[128,128]{0,1:T(8,128)(2,1)S(1)}, u32[]{:S(2)}, u32[]{:S(2)}) %collective-permute-start.3) | collective-permute-done | bytes 32800 | tf_op jit(solution)/shard_map/ppermute | solution.py:22
  49.8 0.4 fusion.46
  50.2 0.3 copy.55
  50.5 0.3 copy.57
  50.7 0.3 copy.56
  51.0 0.2 fusion.54
  51.3 13.5 %fusion.25 = f32[128,16,512]{0,2,1:T(8,128)} fusion(f32[16,512]{1,0:T(8,128)S(1)} %broadcast_in_dim.59, s32[16,512]{1,0:T(8,128)S(1)} %get-tuple-element.59, f32[16,512]{1,0:T(8,128)S(1)} %broadcast_in_dim.57, s32[16,512]{1,0:T(8,128)S(1)} %get-tuple-element.58, f32[16,512]{1,0:T(8,128)S(1)} %broadcast_in_dim.54, s32[16,512]{1,0:T(8,128)S(1)} %get-tuple-element.57, ...), kind=kOutput, calls=%fused_computation.32 | convolution fusion | flops 830472192 | bytes 5963776 | tf_op jit(solution)/shard_map/rcp,cpj->rcj/dot_general | solution.py:101
  64.7 5.5 %copy.47 = f32[128,16,512]{2,1,0:T(8,128)} copy(f32[128,16,512]{0,2,1:T(8,128)} %fusion.25) | data formatting | bytes 8388608 | tf_op jit(solution)/shard_map/rcp,cpj->rcj/transpose | solution.py:101
  70.2 5.1 %reshape.178 = f32[8,16,8192]{2,1,0:T(8,128)} reshape(f32[128,16,512]{2,1,0:T(8,128)} %copy.47) | data formatting | bytes 8388608 | tf_op jit(solution)/shard_map/reshape | solution.py:103
  75.4 0.0 copy-done
  75.4 2.6 %fusion.18 = bf16[16,8192]{1,0:T(8,128)(2,1)S(1)} fusion(f32[8,16,8192]{2,1,0:T(8,128)} %reshape.178, bf16[8,16,8192]{2,1,0:T(8,128)(2,1)S(1)} %copy-done), kind=kLoop, calls=%fused_computation.25 | loop fusion | flops 3014656 | bytes 6553600 | tf_op jit(solution)/shard_map/reduce_sum | solution.py:102
  78.0 0.2 copy.60
  78.2 0.2 copy.48
  78.3 18.7 %all_to_all.5 = bf16[8,16,1024]{2,1,0:T(8,128)(2,1)S(1)} all-to-all(bf16[8,16,1024]{2,1,0:T(8,128)(2,1)S(1)} %copy.48), channel_id=1, replica_groups=mesh['space'=32,'mem'=8] {'mem'}, dimensions={0} | all-to-all | bytes 524288 | tf_op jit(solution)/shard_map/all_to_all | solution.py:34
  97.1 0.6 broadcast_multiply_fusion
  (14 shorter events, 0.2 us)
Async XLA Ops:
  20.7 10.2 %collective-permute-start = (bf16[128,1152]{1,0:T(8,128)(2,1)S(1)}, bf16[128,1152]{1,0:T(8,128)(2,1)S(1)}, u32[]{:S(2)}, u32[]{:S(2)}) collective-permute-start(bf16[128,1152]{1,0:T(8,128)(2,1)S(1)} %get-tuple-element.53), channel_id=1, source_target_pairs={{0,8},{8,16},{16,24},{24,32},{32,40},{40,48},{48,56},{56,64},{64,7... | collective-permute-start | bytes 884744 | tf_op jit(solution)/shard_map/ppermute | solution.py:19
  22.7 10.0 %collective-permute-start.1 = (bf16[128,1152]{1,0:T(8,128)(2,1)S(1)}, bf16[128,1152]{1,0:T(8,128)(2,1)S(1)}, u32[]{:S(2)}, u32[]{:S(2)}) collective-permute-start(bf16[128,1152]{1,0:T(8,128)(2,1)S(1)} %get-tuple-element.54), channel_id=1, source_target_pairs={{8,0},{16,8},{24,16},{32,24},{40,32},{48,40},{56,48},{64,56},{72,6... | collective-permute-start | bytes 884744 | tf_op jit(solution)/shard_map/ppermute | solution.py:22
  35.0 2.4 %slice-start = ((s8[4718592]{0:T(1024)(128)(4,1)}), s8[4194304]{0:T(1024)(128)(4,1)S(1)}, s32[]{:S(2)}) async-start(s8[4718592]{0:T(1024)(128)(4,1)} %bitcast.60), calls=%async_computation.1 | async-start | bytes 8388608
  35.1 0.8 copy-start.1
  35.4 2.0 %slice-start.1 = ((s8[4718592]{0:T(1024)(128)(4,1)}), s8[524288]{0:T(1024)(128)(4,1)S(1)}, s32[]{:S(2)}) async-start(s8[4718592]{0:T(1024)(128)(4,1)} %bitcast.60), calls=%async_computation.2 | async-start | bytes 1048576
  40.3 8.0 %collective-permute-start.2 = (bf16[128,128]{0,1:T(8,128)(2,1)S(1)}, bf16[128,128]{0,1:T(8,128)(2,1)S(1)}, u32[]{:S(2)}, u32[]{:S(2)}) collective-permute-start(bf16[128,128]{0,1:T(8,128)(2,1)S(1)} %get-tuple-element.55), channel_id=1, source_target_pairs={{0,8},{8,16},{16,24},{24,32},{32,40},{40,48},{48,56},{56,64},{64,7... | collective-permute-start | bytes 98312 | tf_op jit(solution)/shard_map/ppermute | solution.py:19
  42.2 7.5 %collective-permute-start.3 = (bf16[128,128]{0,1:T(8,128)(2,1)S(1)}, bf16[128,128]{0,1:T(8,128)(2,1)S(1)}, u32[]{:S(2)}, u32[]{:S(2)}) collective-permute-start(bf16[128,128]{0,1:T(8,128)(2,1)S(1)} %get-tuple-element.56), channel_id=1, source_target_pairs={{8,0},{16,8},{24,16},{32,24},{40,32},{48,40},{56,48},{64,56},{72,6... | collective-permute-start | bytes 98312 | tf_op jit(solution)/shard_map/ppermute | solution.py:22
  70.2 5.1 %copy-start = (bf16[8,16,8192]{2,1,0:T(8,128)(2,1)S(1)}, bf16[8,16,8192]{2,1,0:T(8,128)(2,1)}, u32[]{:S(2)}) copy-start(bf16[8,16,8192]{2,1,0:T(8,128)(2,1)} %param.13) | copy-start | bytes 6291460
where the time goes:
time: 98.4 us; the launch traced here: 97.8 us
  matrix products  31.8 us (32%)
  blocking collectives  18.7 us (19%)
  local copies, waits for them, and re-layouts  17.1 us (17%)
  starting transfers between devices  15.7 us (16%)
  other arithmetic  9.8 us (10%)
  waiting for transfers between devices  4.23 us (4%)
    all_to_all x1, blocking collectives, summed_on_arrival(): lax.all_to_all(pieces, axis, split_axis=0, concat_axis=0, tiled=True)  18.7 us
    dot_general x1, matrix products, shards(): window = jnp.einsum('rcj,cpj->rcp', weighted, table)  14.1 us
    dot_general x1, matrix products, shards(): returned = jnp.einsum('rcp,cpj->rcj', windows, table)  13.5 us
    ppermute x2, starting transfers between devices, with_halo(): lax.ppermute(lax.slice_in_dim(block, 0, width, axis=dim), axis, backward)  11.9 us
    transpose x1, local copies, waits for them, and re-layouts, shards(): returned = jnp.einsum('rcp,cpj->rcj', windows, table)  5.51 us
    reshape x1, local copies, waits for them, and re-layouts, shards(): returned.reshape(mem_dev, n_fields, columns)  5.12 us
    ppermute x2, starting transfers between devices, with_halo(): lax.ppermute(lax.slice_in_dim(block, block.shape[dim] - width, None, axis...  3.84 us
    ppermute x2, waiting for transfers between devices, with_halo(): lax.ppermute(lax.slice_in_dim(block, 0, width, axis=dim), axis, backward)  3.14 us
  transfers between devices with their start and end apart: 4, of which 3 were waited for; matrix products, arithmetic and copies ran while one was open for 1% of the time, Pallas kernels for 0%

commit v1 on v0

v1 whole, which is shorter than its diff:
```python
import jax
import jax.numpy as jnp
from jax import lax
from jax.experimental import pallas as pl
from jax.experimental.pallas import tpu as pltpu
from jax.sharding import PartitionSpec as P

MESH = pl.DeviceIdType.MESH
BLOCK = 128
INTP = 3
SUB_DEV = 2048
NB = 9
HB = 8
CB = 512
NCB = 16
WIN = 384
GREET = 2
F32 = jnp.float32
BF16 = jnp.bfloat16


def dedupe(i0, i1, i2, w0, w1, w2):
    same01, same02, same12 = i0 == i1, i0 == i2, i1 == i2
    zero = jnp.zeros_like(w0)
    none = jnp.full_like(i0, 512.0)
    w0 = w0 + jnp.where(same01, w1, zero) + jnp.where(same02, w2, zero)
    w1 = w1 + jnp.where(same12, w2, zero)
    return i0, jnp.where(same01, none, i1), jnp.where(same02 | same12, none, i2), w0, w1, w2


def build_table(cb, idx_v, wgt_v, table):
    iota = lax.broadcasted_iota(jnp.int32, (16, BLOCK), 0).astype(F32)
    for t in range(CB // BLOCK):
        cols = pl.ds(pl.multiple_of(cb * CB + t * BLOCK, BLOCK), BLOCK)
        idx = [(idx_v[k : k + 1, cols] - (cb * BLOCK + WIN // 2)).astype(F32) for k in range(INTP)]
        wgt = [wgt_v[k : k + 1, cols] for k in range(INTP)]
        rows = [jnp.broadcast_to(v, (16, BLOCK)).astype(BF16) for v in dedupe(*idx, *wgt)]
        i0, i1, i2, w0, w1, w2 = rows
        for r in range(WIN // 16):
            if r * 16 + 16 <= 32 * t or r * 16 >= 32 * t + 288:
                val = jnp.zeros((16, BLOCK), BF16)
            else:
                point = (iota + (r * 16 - WIN // 2)).astype(BF16)
                val = jnp.where(i2 == point, w2, jnp.zeros((16, BLOCK), BF16))
                val = jnp.where(i1 == point, w1, val)
                val = jnp.where(i0 == point, w0, val)
            table[r * 16 : r * 16 + 16, t * BLOCK : (t + 1) * BLOCK] = val


def kernel(
    n_space,
    n_mem,
    inc_h,
    anom_h,
    idx_h,
    wgt_h,
    nb_h,
    tiles_h,
    out_ref,
    inc_v,
    anom_v,
    idx_v,
    wgt_v,
    nb_s,
    tiles_v,
    table_l,
    table_r,
    carry_l,
    carry_r,
    edge,
    spread,
    recv_l,
    recv_r,
    sub,
    smooth,
    part,
    zrecv,
    own,
    in_sem,
    anom_sem,
    tile_sem,
    send_l_sem,
    send_r_sem,
    recv_l_sem,
    recv_r_sem,
    smooth_send_sem,
    smooth_recv_sem,
    z_send_sem,
    z_recv_sem,
):
    me = lax.axis_index("space")
    z = lax.axis_index("mem")
    left, right = me - 1, me + 1
    has_left, has_right = me > 0, me < n_space - 1
    half = NCB // 2

    loads = [
        pltpu.make_async_copy(idx_h, idx_v, in_sem.at[0]),
        pltpu.make_async_copy(wgt_h, wgt_v, in_sem.at[1]),
        pltpu.make_async_copy(inc_h, inc_v, in_sem.at[2]),
        pltpu.make_async_copy(nb_h, nb_s, in_sem.at[3]),
    ]
    for c in loads:
        c.start()

    def anom_copy(cb):
        cols = pl.ds(pl.multiple_of(cb * CB, CB), CB)
        return pltpu.make_async_copy(anom_h.at[:, cols], anom_v.at[:, cols], anom_sem.at[cb])

    for k in range(half):
        anom_copy(k).start()
        anom_copy(NCB - 1 - k).start()

    def tile_copy(b):
        return pltpu.make_async_copy(tiles_h.at[b], tiles_v.at[b], tile_sem.at[b])

    for d in range(half):
        tile_copy(half - 1 - d).start()
        tile_copy(half + d).start()

    barrier = pltpu.get_barrier_semaphore()

    @pl.when(has_left)
    def _():
        pl.semaphore_signal(barrier, inc=1, device_id={"space": left}, device_id_type=MESH)

    @pl.when(has_right)
    def _():
        pl.semaphore_signal(barrier, inc=1, device_id={"space": right}, device_id_type=MESH)

    for off in range(1, n_mem):
        pl.semaphore_signal(
            barrier, inc=1, device_id={"mem": lax.rem(z + off, n_mem)}, device_id_type=MESH
        )

    def to_left(k):
        return pltpu.make_async_remote_copy(
            src_ref=spread.at[k],
            dst_ref=recv_r.at[k],
            send_sem=send_l_sem.at[k],
            recv_sem=recv_r_sem.at[k],
            device_id={"space": left},
            device_id_type=MESH,
        )

    def to_right(k):
        return pltpu.make_async_remote_copy(
            src_ref=spread.at[17 - k],
            dst_ref=recv_l.at[k],
            send_sem=send_r_sem.at[k],
            recv_sem=recv_l_sem.at[k],
            device_id={"space": right},
            device_id_type=MESH,
        )

    def send_pair(k):
        @pl.when(has_left)
        def _():
            to_left(k).start()

        @pl.when(has_right)
        def _():
            to_right(k).start()

    for c in loads:
        c.wait()
    carry_l[...] = jnp.zeros_like(carry_l)
    carry_r[...] = jnp.zeros_like(carry_r)

    def spread_window(cb, table):
        cols = pl.ds(pl.multiple_of(cb * CB, CB), CB)
        inc = inc_v[:, cols].astype(BF16)
        weighted = (anom_v[:, cols].reshape(8, 16, CB) * inc[None]).reshape(128, CB)
        return lax.dot_general(
            weighted, table[...], (((1,), (1,)), ((), ())), preferred_element_type=F32
        )

    def spread_step(k, greet):
        cl, cr = k, NCB - 1 - k
        anom_copy(cl).wait()
        anom_copy(cr).wait()
        build_table(cl, idx_v, wgt_v, table_l.at[k])
        build_table(cr, idx_v, wgt_v, table_r.at[k])
        win_l = spread_window(cl, table_l.at[k])
        win_r = spread_window(cr, table_r.at[k])
        done_l = win_l[:, :128] + carry_l[0]
        done_r = win_r[:, 256:] + carry_r[0]
        carry_l[0] = win_l[:, 128:256] + carry_l[1]
        carry_r[0] = win_r[:, 128:256] + carry_r[1]
        carry_l[1] = win_l[:, 256:]
        carry_r[1] = win_r[:, :128]
        spread[k] = done_l.astype(BF16)
        spread[17 - k] = done_r.astype(BF16)
        return done_l, done_r

    for k in range(GREET):
        done_l, done_r = spread_step(k, False)
        if k < 2:
            edge[k] = done_l
            edge[3 - k] = done_r

    pl.semaphore_wait(barrier, n_mem - 1 + has_left.astype(jnp.int32) + has_right.astype(jnp.int32))

    for k in range(GREET):
        send_pair(k)

    def spread_loop(k, carry):
        done_l, done_r = spread_step(k, False)
        sub[7 + k] = done_l.astype(BF16)
        sub[24 - k] = done_r.astype(BF16)
        send_pair(k)
        return carry

    lax.fori_loop(GREET, half, spread_loop, 0)
    mid_l = (carry_l[0] + carry_r[1]).astype(BF16)
    mid_r = (carry_l[1] + carry_r[0]).astype(BF16)
    spread[8] = mid_l
    spread[9] = mid_r
    sub[15] = mid_l
    sub[16] = mid_r
    send_pair(8)

    def conv(b):
        tile_copy(b).wait()
        picked = jnp.concatenate([sub[nb_s[n, b]] for n in range(NB)], axis=1)
        value = jnp.dot(picked, tiles_v[b], preferred_element_type=F32)
        smooth[1 + b] = value.astype(BF16)

    def interp(cb, table):
        window = jnp.concatenate([smooth[cb], smooth[cb + 1], smooth[cb + 2]], axis=1)
        back = jnp.dot(window, table[...], preferred_element_type=F32)
        cols = pl.ds(pl.multiple_of(cb * CB, CB), CB)
        prod = back * anom_v[:, cols].astype(F32)
        total = jnp.sum(prod.reshape(8, 16, CB), axis=0)
        owner, h = cb // 2, lax.rem(cb, 2)
        part[cb] = total.astype(BF16)

        @pl.when(owner == z)
        def _():
            own[h] = total

        @pl.when(owner != z)
        def _():
            z_copy(cb).start()

    def z_copy(cb):
        owner, h = cb // 2, lax.rem(cb, 2)
        return pltpu.make_async_remote_copy(
            src_ref=part.at[cb],
            dst_ref=zrecv.at[z, h],
            send_sem=z_send_sem.at[cb],
            recv_sem=z_recv_sem.at[z, h],
            device_id={"mem": owner},
            device_id_type=MESH,
        )

    @pl.when(has_left)
    def _():
        to_right(0).wait_recv()
        sub[8] = (edge[1] + recv_l[0].astype(F32)).astype(BF16)
        to_right(1).wait_recv()
        sub[7] = (edge[0] + recv_l[1].astype(F32)).astype(BF16)

    @pl.when(jnp.logical_not(has_left))
    def _():
        sub[8] = edge[1].astype(BF16)
        sub[0:8] = jnp.zeros((8, 128, 128), BF16)

    @pl.when(has_right)
    def _():
        to_left(0).wait_recv()
        sub[23] = (edge[2] + recv_r[0].astype(F32)).astype(BF16)
        to_left(1).wait_recv()
        sub[24] = (edge[3] + recv_r[1].astype(F32)).astype(BF16)

    @pl.when(jnp.logical_not(has_right))
    def _():
        sub[23] = edge[2].astype(BF16)
        sub[24:32] = jnp.zeros((8, 128, 128), BF16)

    conv(half - 1)
    conv(half)

    def conv_loop(d, carry):
        @pl.when(has_left)
        def _():
            to_right(d).wait_recv()
            sub[8 - d] = recv_l[d]

        @pl.when(has_right)
        def _():
            to_left(d).wait_recv()
            sub[23 + d] = recv_r[d]

        conv(half - d)
        conv(half - 1 + d)
        return carry

    lax.fori_loop(2, half + 1, conv_loop, 0)

    smooth_left = pltpu.make_async_remote_copy(
        src_ref=smooth.at[1],
        dst_ref=smooth.at[17],
        send_sem=smooth_send_sem.at[0],
        recv_sem=smooth_recv_sem.at[0],
        device_id={"space": left},
        device_id_type=MESH,
    )
    smooth_right = pltpu.make_async_remote_copy(
        src_ref=smooth.at[16],
        dst_ref=smooth.at[0],
        send_sem=smooth_send_sem.at[1],
        recv_sem=smooth_recv_sem.at[1],
        device_id={"space": right},
        device_id_type=MESH,
    )

    @pl.when(has_left)
    def _():
        smooth_left.start()

    @pl.when(has_right)
    def _():
        smooth_right.start()

    def interp_loop(s, carry):
        k = half - 1 - s
        interp(k, table_l.at[k])
        interp(NCB - 1 - k, table_r.at[k])
        return carry

    lax.fori_loop(0, half - 1, interp_loop, 0)

    @pl.when(has_left)
    def _():
        smooth_right.wait_recv()

    @pl.when(has_right)
    def _():
        smooth_left.wait_recv()

    @pl.when(jnp.logical_not(has_left))
    def _():
        smooth[0] = jnp.zeros((128, 128), BF16)

    @pl.when(jnp.logical_not(has_right))
    def _():
        smooth[17] = jnp.zeros((128, 128), BF16)

    interp(0, table_l.at[0])
    interp(NCB - 1, table_r.at[0])

    @pl.when(has_left)
    def _():
        for k in range(9):
            to_left(k).wait_send()
        smooth_left.wait_send()

    @pl.when(has_right)
    def _():
        for k in range(9):
            to_right(k).wait_send()
        smooth_right.wait_send()

    def z_arrived(source, h):
        return pltpu.make_async_remote_copy(
            src_ref=part.at[0],
            dst_ref=zrecv.at[source, h],
            send_sem=z_send_sem.at[0],
            recv_sem=z_recv_sem.at[source, h],
            device_id={"mem": source},
            device_id_type=MESH,
        )

    for h in range(2):
        total = own[h]
        for off in range(1, n_mem):
            source = lax.rem(z + off, n_mem)
            z_arrived(source, h).wait_recv()
            total = total + zrecv[source, h].astype(F32)
        out_ref[:, h * CB : (h + 1) * CB] = total * (1.0 / (8 * n_mem - 1))

    for cb in range(NCB):
        @pl.when(cb // 2 != z)
        def _():
            z_copy(cb).wait_send()


def shards(increment, anomalies, interp_index, interp_weight, neighbour_blocks, tiles):
    n_space, n_mem = lax.axis_size("space"), lax.axis_size("mem")
    anomalies = anomalies.reshape(128, NCB * CB)
    tiles = tiles.reshape(16, NB * BLOCK, BLOCK)
    hbm = pl.BlockSpec(memory_space=pl.ANY)
    vmem = pltpu.VMEM
    dma = pltpu.SemaphoreType.DMA
    return pl.pallas_call(
        lambda *refs: kernel(n_space, n_mem, *refs),
        out_shape=jax.ShapeDtypeStruct((16, 2 * CB), F32),
        in_specs=[hbm] * 6,
        out_specs=pl.BlockSpec(memory_space=pltpu.VMEM),
        scratch_shapes=[
            vmem((16, NCB * CB), F32),
            vmem((128, NCB * CB), BF16),
            vmem((INTP, NCB * CB), jnp.int32),
            vmem((INTP, NCB * CB), F32),
            pltpu.SMEM((NB, 16), jnp.int32),
            vmem((16, NB * BLOCK, BLOCK), BF16),
            vmem((8, WIN, CB), BF16),
            vmem((8, WIN, CB), BF16),
            vmem((2, 128, 128), F32),
            vmem((2, 128, 128), F32),
            vmem((4, 128, 128), F32),
            vmem((18, 128, 128), BF16),
            vmem((9, 128, 128), BF16),
            vmem((9, 128, 128), BF16),
            vmem((32, 128, 128), BF16),
            vmem((18, 128, 128), BF16),
            vmem((NCB, 16, CB), BF16),
            vmem((8, 2, 16, CB), BF16),
            vmem((2, 16, CB), F32),
            dma((4,)),
            dma((NCB,)),
            dma((16,)),
            dma((9,)),
            dma((9,)),
            dma((9,)),
            dma((9,)),
            dma((2,)),
            dma((2,)),
            dma((NCB,)),
            dma((8, 2)),
        ],
        compiler_params=pltpu.CompilerParams(
            collective_id=0, has_side_effects=True, vmem_limit_bytes=67_043_328
        ),
        name="nicas",
    )(increment, anomalies, interp_index, interp_weight, neighbour_blocks, tiles)


def solution(mesh):
    in_specs = (
        P(None, "space"),
        P("mem", None, "space"),
        P(None, "space"),
        P(None, "space"),
        P(None, "space"),
        P("space", None, None, None),
    )
    out_specs = P(None, ("space", "mem"))
    return jax.shard_map(shards, mesh=mesh, in_specs=in_specs, out_specs=out_specs, check_vma=False)
```

time: 98.4 us -> 31 us (0.32)
  matrix products: 31.8 us -> 0 us
  Pallas kernels: 0 us -> 29.1 us
  blocking collectives: 18.7 us -> 0 us
  starting transfers between devices: 15.7 us -> 0 us
  local copies, waits for them, and re-layouts: 17.1 us -> 1.47 us
  other arithmetic: 9.8 us -> 0 us
  waiting for transfers between devices: 4.23 us -> 0 us
    dot_general x4 -> x0, matrix products: 31.8 us -> none  [the longest x1 14.1 us: shards(): window = jnp.einsum('rcj,cpj->rcp', weighted, table)]
    pallas_call x0 -> x1, Pallas kernels: none -> 29.1 us  [shards(): pl.pallas_call(lambda *refs: kernel(n_space, n_mem, *refs), out_shape=jax...]
    all_to_all x1 -> x0, blocking collectives: 18.7 us -> none  [summed_on_arrival(): lax.all_to_all(pieces, axis, split_axis=0, concat_axis=0, tiled=True)]
    ppermute x4 -> x0, starting transfers between devices: 15.7 us -> none  [the longest x2 11.9 us: with_halo(): lax.ppermute(lax.slice_in_dim(block, 0, width, axis=dim), axis, backward)]
    transpose x2 -> x0, local copies, waits for them, and re-layouts: 5.66 us -> none  [the longest x1 5.51 us: shards(): returned = jnp.einsum('rcp,cpj->rcj', windows, table)]
    reshape x1 -> x0, local copies, waits for them, and re-layouts: 5.12 us -> none  [shards(): returned.reshape(mem_dev, n_fields, columns)]
    ppermute x4 -> x0, waiting for transfers between devices: 4.23 us -> none  [the longest x2 3.14 us: with_halo(): lax.ppermute(lax.slice_in_dim(block, 0, width, axis=dim), axis, backward)]
    slice x5 -> x0, local copies, waits for them, and re-layouts: 3.05 us -> none  [the longest x1 1.33 us: interp_table(): weight_blocks[which][:, None, :]]
  transfers between devices with their start and end apart: 4 -> 0, of which waited for: 3 -> 0; matrix products, arithmetic and copies ran while one was open for 1% -> 0% of each run, Pallas kernels for 0% -> 0%
where the time goes in v1:
time: 31 us; the launch traced here: 30.6 us
  Pallas kernels  29.1 us (94%)
  local copies, waits for them, and re-layouts  1.47 us (5%)
    pallas_call x1, Pallas kernels, shards(): pl.pallas_call(lambda *refs: kernel(n_space, n_mem, *refs), out_shape=jax...  29.1 us
    unnamed x1, local copies, waits for them, and re-layouts  1.47 us

profile of v1, /device:TPU:2, one launch (start us, length us, event | category | flops | bytes accessed | tf_op | source)
XLA Modules:
  0.0 30.6 jit_solution(6989706637398120825)
XLA Ops:
  0.0 29.1 %nicas.1 = f32[16,1024]{1,0:T(8,128)} custom-call(f32[16,8192]{1,0:T(8,128)} %refs_0_.1, bf16[128,8192]{1,0:T(8,128)(2,1)} %bitcast.3, s32[3,8192]{1,0:T(4,128)} %refs_2_.1, f32[3,8192]{1,0:T(4,128)} %refs_3_.1, s32[9,16]{1,0:T(8,128)} %refs_4_.1, bf16[16,1152,128]{2,1,0:T(8,128)(2,1)} %bitcast.2), custom_call_target="tpu_custom_call" | custom-call | tf_op jit(solution)/shard_map/nicas/pallas_call | solution.py:396
  29.1 1.5 %copy.8 = f32[16,1024]{1,0:T(8,128)} copy(f32[16,1024]{1,0:T(8,128)} %nicas.1) | data formatting | bytes 131072

commit v2 on v1

v2 whole, which is shorter than its diff:
```python
import jax
import jax.numpy as jnp
from jax import lax
from jax.experimental import pallas as pl
from jax.experimental.pallas import tpu as pltpu
from jax.sharding import PartitionSpec as P

MESH = pl.DeviceIdType.MESH
BLOCK = 128
INTP = 3
SUB_DEV = 2048
NB = 9
HB = 8
CB = 512
NCB = 16
WIN = 384
GREET = 2
FIRST = 2
EARLY = 3
F32 = jnp.float32
BF16 = jnp.bfloat16


def dedupe(i0, i1, i2, w0, w1, w2):
    same01, same02, same12 = i0 == i1, i0 == i2, i1 == i2
    zero = jnp.zeros_like(w0)
    none = jnp.full_like(i0, 512.0)
    w0 = w0 + jnp.where(same01, w1, zero) + jnp.where(same02, w2, zero)
    w1 = w1 + jnp.where(same12, w2, zero)
    return i0, jnp.where(same01, none, i1), jnp.where(same02 | same12, none, i2), w0, w1, w2


def build_table(cb, idx_v, wgt_v, table):
    iota = lax.broadcasted_iota(jnp.int32, (16, BLOCK), 0).astype(F32)
    for t in range(CB // BLOCK):
        cols = slice(cb * CB + t * BLOCK, cb * CB + (t + 1) * BLOCK)
        idx = [(idx_v[k : k + 1, cols] - (cb * BLOCK + WIN // 2)).astype(F32) for k in range(INTP)]
        wgt = [wgt_v[k : k + 1, cols] for k in range(INTP)]
        rows = [jnp.broadcast_to(v, (16, BLOCK)).astype(BF16) for v in dedupe(*idx, *wgt)]
        i0, i1, i2, w0, w1, w2 = rows
        for r in range(WIN // 16):
            if r * 16 + 16 <= 32 * t or r * 16 >= 32 * t + 288:
                val = jnp.zeros((16, BLOCK), BF16)
            else:
                point = (iota + (r * 16 - WIN // 2)).astype(BF16)
                val = jnp.where(i2 == point, w2, jnp.zeros((16, BLOCK), BF16))
                val = jnp.where(i1 == point, w1, val)
                val = jnp.where(i0 == point, w0, val)
            table[r * 16 : r * 16 + 16, t * BLOCK : (t + 1) * BLOCK] = val


def kernel(
    n_space,
    n_mem,
    inc_h,
    anom_h,
    idx_h,
    wgt_h,
    nb_h,
    tiles_h,
    out_ref,
    inc_v,
    anom_v,
    idx_v,
    wgt_v,
    nb_s,
    tiles_v,
    table_l,
    table_r,
    spread,
    recv_l,
    recv_r,
    sub,
    smooth,
    part,
    zrecv,
    in_sem,
    send_l_sem,
    send_r_sem,
    recv_l_sem,
    recv_r_sem,
    smooth_send_sem,
    smooth_recv_sem,
    z_send_sem,
    z_recv_sem,
    near_sem,
    far_sem,
):
    me = lax.axis_index("space")
    z = lax.axis_index("mem")
    left, right = me - 1, me + 1
    has_left, has_right = me > 0, me < n_space - 1
    half = NCB // 2

    lo, hi = FIRST * CB, (NCB - FIRST) * CB
    first = [
        pltpu.make_async_copy(idx_h, idx_v, in_sem.at[0]),
        pltpu.make_async_copy(wgt_h, wgt_v, in_sem.at[1]),
        pltpu.make_async_copy(inc_h, inc_v, in_sem.at[2]),
        pltpu.make_async_copy(anom_h.at[:, :lo], anom_v.at[:, :lo], in_sem.at[3]),
        pltpu.make_async_copy(anom_h.at[:, hi:], anom_v.at[:, hi:], in_sem.at[4]),
    ]
    second = pltpu.make_async_copy(anom_h.at[:, lo:hi], anom_v.at[:, lo:hi], in_sem.at[5])
    third = [
        pltpu.make_async_copy(nb_h, nb_s, in_sem.at[6]),
        pltpu.make_async_copy(tiles_h, tiles_v, in_sem.at[7]),
    ]
    for c in (*first, second, *third):
        c.start()

    barrier = pltpu.get_barrier_semaphore()

    def greet(sem, **peer):
        pl.semaphore_signal(sem, inc=1, device_id=peer, device_id_type=MESH)

    def around(step):
        return lax.rem(z + step, n_mem), lax.rem(z + n_mem - step, n_mem)

    for peer in around(1):
        greet(barrier, mem=peer)

    @pl.when(has_left)
    def _():
        greet(barrier, space=left)

    @pl.when(has_right)
    def _():
        greet(barrier, space=right)

    def to_left(k):
        return pltpu.make_async_remote_copy(
            src_ref=spread.at[k],
            dst_ref=recv_r.at[k],
            send_sem=send_l_sem.at[k],
            recv_sem=recv_r_sem.at[k],
            device_id={"space": left},
            device_id_type=MESH,
        )

    def to_right(k):
        return pltpu.make_async_remote_copy(
            src_ref=spread.at[17 - k],
            dst_ref=recv_l.at[k],
            send_sem=send_r_sem.at[k],
            recv_sem=recv_l_sem.at[k],
            device_id={"space": right},
            device_id_type=MESH,
        )

    def send_pair(k):
        @pl.when(has_left)
        def _():
            to_left(k).start()

        @pl.when(has_right)
        def _():
            to_right(k).start()

    def spread_window(cb, table):
        cols = slice(cb * CB, (cb + 1) * CB)
        build_table(cb, idx_v, wgt_v, table)
        inc = inc_v[:, cols].astype(BF16)
        weighted = (anom_v[:, cols].reshape(8, 16, CB) * inc[None]).reshape(128, CB)
        return lax.dot_general(
            weighted, table[...], (((1,), (1,)), ((), ())), preferred_element_type=F32
        )

    for c in first:
        c.wait()
    carry_l = [None, None]
    carry_r = [None, None]
    edge_l, edge_r = [], []

    def plus(a, b):
        return a if b is None else a + b

    for k in range(half):
        if k == FIRST:
            second.wait()
        win_l = spread_window(k, table_l.at[k])
        win_r = spread_window(NCB - 1 - k, table_r.at[k])
        done_l = plus(win_l[:, :128], carry_l[0])
        done_r = plus(win_r[:, 256:], carry_r[0])
        carry_l = [plus(win_l[:, 128:256], carry_l[1]), win_l[:, 256:]]
        carry_r = [plus(win_r[:, 128:256], carry_r[1]), win_r[:, :128]]
        spread[k] = done_l.astype(BF16)
        spread[17 - k] = done_r.astype(BF16)
        if k >= 2:
            sub[7 + k] = done_l.astype(BF16)
            sub[24 - k] = done_r.astype(BF16)
        if k == GREET - 1:
            pl.semaphore_wait(barrier, 2 + has_left.astype(jnp.int32) + has_right.astype(jnp.int32))
            for peer in around(1):
                greet(near_sem, mem=peer)
            for early in range(GREET):
                send_pair(early)
        if k >= GREET:
            send_pair(k)
    mid_l = (carry_l[0] + carry_r[1]).astype(BF16)
    mid_r = (carry_l[1] + carry_r[0]).astype(BF16)
    spread[8] = mid_l
    spread[9] = mid_r
    send_pair(8)
    sub[15] = mid_l
    sub[16] = mid_r

    pl.semaphore_wait(near_sem, 2)
    for peer in around(2):
        greet(far_sem, mem=peer)

    def conv(b):
        picked = jnp.concatenate([sub[nb_s[n, b]] for n in range(NB)], axis=1)
        value = jnp.dot(picked, tiles_v[b], preferred_element_type=F32)
        smooth[1 + b] = value.astype(BF16)

    def z_copy(cb):
        owner, h = cb // 2, cb % 2
        return pltpu.make_async_remote_copy(
            src_ref=part.at[cb],
            dst_ref=zrecv.at[z, h],
            send_sem=z_send_sem.at[cb],
            recv_sem=z_recv_sem.at[z, h],
            device_id={"mem": owner},
            device_id_type=MESH,
        )

    def interp(cb, table):
        window = jnp.concatenate([smooth[cb], smooth[cb + 1], smooth[cb + 2]], axis=1)
        back = jnp.dot(window, table[...], preferred_element_type=F32)
        cols = slice(cb * CB, (cb + 1) * CB)
        prod = back * anom_v[:, cols].astype(F32)
        part[cb] = jnp.sum(prod.reshape(8, 16, CB), axis=0).astype(BF16)

        @pl.when(cb // 2 != z)
        def _():
            z_copy(cb).start()

    def interp_pair(k):
        interp(k, table_l.at[k])
        interp(NCB - 1 - k, table_r.at[k])

    for c in third:
        c.wait()

    def halo(side, copy, own, at, recv, d):
        @pl.when(side)
        def _():
            copy(d).wait_recv()
            if d < 2:
                sub[at] = (own[...].astype(F32) + recv[d].astype(F32)).astype(BF16)
            else:
                sub[at] = recv[d]

        @pl.when(jnp.logical_not(side))
        def _():
            sub[at] = own[...] if d == 0 else jnp.zeros((128, 128), BF16)

    for d in range(half + 1):
        halo(has_left, to_right, spread.at[1 - d] if d < 2 else None, 8 - d, recv_l, d)
        halo(has_right, to_left, spread.at[16 + d] if d < 2 else None, 23 + d, recv_r, d)
        if d >= 1:
            if d == half:
                pl.semaphore_wait(far_sem, 2)
                for s in range(EARLY):
                    interp_pair(half - 1 - s)
            conv(half - d)
            conv(half - 1 + d)

    smooth_left = pltpu.make_async_remote_copy(
        src_ref=smooth.at[1],
        dst_ref=smooth.at[17],
        send_sem=smooth_send_sem.at[0],
        recv_sem=smooth_recv_sem.at[0],
        device_id={"space": left},
        device_id_type=MESH,
    )
    smooth_right = pltpu.make_async_remote_copy(
        src_ref=smooth.at[16],
        dst_ref=smooth.at[0],
        send_sem=smooth_send_sem.at[1],
        recv_sem=smooth_recv_sem.at[1],
        device_id={"space": right},
        device_id_type=MESH,
    )

    @pl.when(has_left)
    def _():
        smooth_left.start()

    @pl.when(has_right)
    def _():
        smooth_right.start()

    for s in range(EARLY, half - 1):
        interp_pair(half - 1 - s)

    @pl.when(has_left)
    def _():
        smooth_right.wait_recv()

    @pl.when(has_right)
    def _():
        smooth_left.wait_recv()

    @pl.when(jnp.logical_not(has_left))
    def _():
        smooth[0] = jnp.zeros((128, 128), BF16)

    @pl.when(jnp.logical_not(has_right))
    def _():
        smooth[17] = jnp.zeros((128, 128), BF16)

    interp_pair(0)

    @pl.when(has_left)
    def _():
        for k in range(9):
            to_left(k).wait_send()
        smooth_left.wait_send()

    @pl.when(has_right)
    def _():
        for k in range(9):
            to_right(k).wait_send()
        smooth_right.wait_send()

    for cb in range(NCB):
        @pl.when(cb // 2 != z)
        def _():
            z_copy(cb).wait_send()

    def z_arrived(source, h):
        return pltpu.make_async_remote_copy(
            src_ref=part.at[0],
            dst_ref=zrecv.at[source, h],
            send_sem=z_send_sem.at[0],
            recv_sem=z_recv_sem.at[source, h],
            device_id={"mem": source},
            device_id_type=MESH,
        )

    for off in range(1, n_mem):
        for h in range(2):
            z_arrived(lax.rem(z + off, n_mem), h).wait_recv()
    for h in range(2):
        total = part[2 * z + h].astype(F32)
        for off in range(1, n_mem):
            total = total + zrecv[lax.rem(z + off, n_mem), h].astype(F32)
        out_ref[:, h * CB : (h + 1) * CB] = total * (1.0 / (8 * n_mem - 1))


def shards(increment, anomalies, interp_index, interp_weight, neighbour_blocks, tiles):
    n_space, n_mem = lax.axis_size("space"), lax.axis_size("mem")
    anomalies = anomalies.reshape(128, NCB * CB)
    tiles = tiles.reshape(16, NB * BLOCK, BLOCK)
    hbm = pl.BlockSpec(memory_space=pl.ANY)
    vmem = pltpu.VMEM
    dma = pltpu.SemaphoreType.DMA
    return pl.pallas_call(
        lambda *refs: kernel(n_space, n_mem, *refs),
        out_shape=jax.ShapeDtypeStruct((16, 2 * CB), F32),
        in_specs=[hbm] * 6,
        out_specs=pl.BlockSpec(memory_space=pltpu.VMEM),
        scratch_shapes=[
            vmem((16, NCB * CB), F32),
            vmem((128, NCB * CB), BF16),
            vmem((INTP, NCB * CB), jnp.int32),
            vmem((INTP, NCB * CB), F32),
            pltpu.SMEM((NB, 16), jnp.int32),
            vmem((16, NB * BLOCK, BLOCK), BF16),
            vmem((8, WIN, CB), BF16),
            vmem((8, WIN, CB), BF16),
            vmem((18, 128, 128), BF16),
            vmem((9, 128, 128), BF16),
            vmem((9, 128, 128), BF16),
            vmem((32, 128, 128), BF16),
            vmem((18, 128, 128), BF16),
            vmem((NCB, 16, CB), BF16),
            vmem((8, 2, 16, CB), BF16),
            dma((8,)),
            dma((9,)),
            dma((9,)),
            dma((9,)),
            dma((9,)),
            dma((2,)),
            dma((2,)),
            dma((NCB,)),
            dma((8, 2)),
            pltpu.SemaphoreType.REGULAR,
            pltpu.SemaphoreType.REGULAR,
        ],
        compiler_params=pltpu.CompilerParams(
            collective_id=0, has_side_effects=True, vmem_limit_bytes=67_043_328
        ),
        name="nicas",
    )(increment, anomalies, interp_index, interp_weight, neighbour_blocks, tiles)


def solution(mesh):
    in_specs = (
        P(None, "space"),
        P("mem", None, "space"),
        P(None, "space"),
        P(None, "space"),
        P(None, "space"),
        P("space", None, None, None),
    )
    out_specs = P(None, ("space", "mem"))
    return jax.shard_map(shards, mesh=mesh, in_specs=in_specs, out_specs=out_specs, check_vma=False)
```

time: 31 us -> 27.7 us (0.89)
  Pallas kernels: 29.1 us -> 26.1 us
    pallas_call x1, Pallas kernels: 29.1 us -> 26.1 us  [shards(): pl.pallas_call(lambda *refs: kernel(n_space, n_mem, *refs), out_shape=jax...]
where the time goes in v2:
time: 27.7 us; the launch traced here: 27.6 us
  Pallas kernels  26.1 us (94%)
  local copies, waits for them, and re-layouts  1.47 us (5%)
    pallas_call x1, Pallas kernels, shards(): pl.pallas_call(lambda *refs: kernel(n_space, n_mem, *refs), out_shape=jax...  26.1 us
    unnamed x1, local copies, waits for them, and re-layouts  1.47 us

profile of v2, /device:TPU:2, one launch (start us, length us, event | category | flops | bytes accessed | tf_op | source)
XLA Modules:
  0.0 27.6 jit_solution(17168305995106522460)
XLA Ops:
  0.0 26.1 %nicas.1 = f32[16,1024]{1,0:T(8,128)} custom-call(f32[16,8192]{1,0:T(8,128)} %refs_0_.1, bf16[128,8192]{1,0:T(8,128)(2,1)} %bitcast.3, s32[3,8192]{1,0:T(4,128)} %refs_2_.1, f32[3,8192]{1,0:T(4,128)} %refs_3_.1, s32[9,16]{1,0:T(8,128)} %refs_4_.1, bf16[16,1152,128]{2,1,0:T(8,128)(2,1)} %bitcast.2), custom_call_target="tpu_custom_call" | custom-call | tf_op jit(solution)/shard_map/nicas/pallas_call | solution.py:359
  26.1 1.5 %copy.8 = f32[16,1024]{1,0:T(8,128)} copy(f32[16,1024]{1,0:T(8,128)} %nicas.1) | data formatting | bytes 131072

commit v3 on v2

v3 whole, which is shorter than its diff:
```python
import jax
import jax.numpy as jnp
from jax import lax
from jax.experimental import pallas as pl
from jax.experimental.pallas import tpu as pltpu
from jax.sharding import PartitionSpec as P

MESH = pl.DeviceIdType.MESH
BLOCK = 128
INTP = 3
SUB_DEV = 2048
NB = 9
CB = 512
NCB = 16
CP = 2 * CB
WIN = 512
BAND = 288
FIRST = 2
EARLY = 3
VMEM_LIMIT = 67_043_328 - 190 * 1024
F32 = jnp.float32
BF16 = jnp.bfloat16


def dedupe(i0, i1, i2, w0, w1, w2):
    same01, same02, same12 = i0 == i1, i0 == i2, i1 == i2
    zero = jnp.zeros_like(w0)
    none = jnp.full_like(i0, 512.0)
    w0 = w0 + jnp.where(same01, w1, zero) + jnp.where(same02, w2, zero)
    w1 = w1 + jnp.where(same12, w2, zero)
    return i0, jnp.where(same01, none, i1), jnp.where(same02 | same12, none, i2), w0, w1, w2


def band(t):
    return range(2 * t, 2 * t + BAND // 16)


def clear_table(table):
    for t in range(0, CP // BLOCK, 2):
        lanes = slice(t * BLOCK, (t + 2) * BLOCK)
        low, high = 32 * t, 32 * t + BAND + 32
        if low:
            table[0:low, lanes] = jnp.zeros((low, 2 * BLOCK), BF16)
        if high < WIN:
            table[high:WIN, lanes] = jnp.zeros((WIN - high, 2 * BLOCK), BF16)


def build_table(cb, idx_v, wgt_v, table):
    iota = lax.broadcasted_iota(jnp.int32, (16, BLOCK), 0).astype(F32)
    zero = jnp.zeros((16, BLOCK), BF16)
    for t in range(0, CP // BLOCK, 2):
        rows = []
        for u in (t, t + 1):
            cols = slice(cb * CB + u * BLOCK, cb * CB + (u + 1) * BLOCK)
            idx = [(idx_v[k : k + 1, cols] - (cb * BLOCK + WIN // 2)).astype(F32) for k in range(INTP)]
            wgt = [wgt_v[k : k + 1, cols] for k in range(INTP)]
            rows.append([jnp.broadcast_to(v, (16, BLOCK)).astype(BF16) for v in dedupe(*idx, *wgt)])
        for r in range(2 * t, 2 * t + BAND // 16 + 2):
            point = (iota + (r * 16 - WIN // 2)).astype(BF16)
            vals = []
            for u, (i0, i1, i2, w0, w1, w2) in zip((t, t + 1), rows):
                val = zero
                if r in band(u):
                    val = jnp.where(i2 == point, w2, zero)
                    val = jnp.where(i1 == point, w1, val)
                    val = jnp.where(i0 == point, w0, val)
                vals.append(val)
            table[r * 16 : r * 16 + 16, t * BLOCK : (t + 2) * BLOCK] = jnp.concatenate(vals, axis=1)


def kernel(
    n_space,
    n_mem,
    inc_h,
    anom_h,
    idx_h,
    wgt_h,
    nb_h,
    tiles_h,
    out_ref,
    inc_v,
    anom_v,
    idx_v,
    wgt_v,
    nb_s,
    tiles_v,
    table_l,
    table_r,
    spread,
    recv_l,
    recv_r,
    sub,
    smooth,
    part,
    zrecv,
    in_sem,
    recv_l_sem,
    recv_r_sem,
    smooth_sem,
    out_sem,
    near_sem,
    far_sem,
):
    me = lax.axis_index("space")
    z = lax.axis_index("mem")
    left, right = me - 1, me + 1
    has_left, has_right = me > 0, me < n_space - 1
    steps = NCB // 4

    barrier = pltpu.get_barrier_semaphore()

    def greet(sem, **peer):
        pl.semaphore_signal(sem, inc=1, device_id=peer, device_id_type=MESH)

    def around(step):
        return lax.rem(z + step, n_mem), lax.rem(z + n_mem - step, n_mem)

    lo, hi = FIRST * CB, (NCB - FIRST) * CB
    first = [
        pltpu.make_async_copy(idx_h, idx_v, in_sem.at[0]),
        pltpu.make_async_copy(wgt_h, wgt_v, in_sem.at[1]),
        pltpu.make_async_copy(inc_h, inc_v, in_sem.at[2]),
        pltpu.make_async_copy(anom_h.at[:, :lo], anom_v.at[:, :lo], in_sem.at[3]),
        pltpu.make_async_copy(anom_h.at[:, hi:], anom_v.at[:, hi:], in_sem.at[4]),
    ]
    second = pltpu.make_async_copy(anom_h.at[:, lo:hi], anom_v.at[:, lo:hi], in_sem.at[5])
    third = [
        pltpu.make_async_copy(nb_h, nb_s, in_sem.at[6]),
        pltpu.make_async_copy(tiles_h, tiles_v, in_sem.at[7]),
    ]
    for c in (*first, second, *third):
        c.start()

    for peer in around(1):
        greet(barrier, mem=peer)

    @pl.when(has_left)
    def _():
        greet(barrier, space=left)

    @pl.when(has_right)
    def _():
        greet(barrier, space=right)

    for i in range(steps):
        clear_table(table_l.at[i])
        clear_table(table_r.at[i])

    def size(i):
        return 2 if i < steps else 1

    def to_left(i):
        blocks = pl.ds(2 * i, size(i))
        return pltpu.make_async_remote_copy(
            src_ref=spread.at[blocks],
            dst_ref=recv_r.at[blocks],
            send_sem=out_sem.at[0],
            recv_sem=recv_r_sem.at[i],
            device_id={"space": left},
            device_id_type=MESH,
        )

    def to_right(i):
        low = 18 - 2 * i - size(i)
        return pltpu.make_async_remote_copy(
            src_ref=spread.at[pl.ds(low, size(i))],
            dst_ref=recv_l.at[pl.ds(low - 9, size(i))],
            send_sem=out_sem.at[1],
            recv_sem=recv_l_sem.at[i],
            device_id={"space": right},
            device_id_type=MESH,
        )

    def send_pair(i):
        @pl.when(has_left)
        def _():
            to_left(i).start()

        @pl.when(has_right)
        def _():
            to_right(i).start()

    def spread_window(cb, table):
        cols = slice(cb * CB, cb * CB + CP)
        build_table(cb, idx_v, wgt_v, table)
        inc = inc_v[:, cols].astype(BF16)
        weighted = (anom_v[:, cols].reshape(8, 16, CP) * inc[None]).reshape(128, CP)
        return [
            lax.dot_general(
                weighted,
                table[h * 256 : (h + 1) * 256, :],
                (((1,), (1,)), ((), ())),
                preferred_element_type=F32,
            )
            for h in range(2)
        ]

    for c in first:
        c.wait()
    carry_l = carry_r = None

    def plus(a, b):
        return a if b is None else a + b

    for i in range(steps):
        if i == FIRST // 2:
            second.wait()
        win_l = spread_window(2 * i, table_l.at[i])
        win_r = spread_window(NCB - 2 - 2 * i, table_r.at[i])
        done_l = plus(win_l[0], carry_l).astype(BF16)
        done_r = plus(win_r[1], carry_r).astype(BF16)
        carry_l, carry_r = win_l[1], win_r[0]
        for h in range(2):
            lanes = slice(h * 128, (h + 1) * 128)
            spread[2 * i + h] = done_l[:, lanes]
            spread[16 - 2 * i + h] = done_r[:, lanes]
            if i:
                sub[7 + 2 * i + h] = done_l[:, lanes]
                sub[23 - 2 * i + h] = done_r[:, lanes]
        if i == 0:
            pl.semaphore_wait(barrier, 2 + has_left.astype(jnp.int32) + has_right.astype(jnp.int32))
            for peer in around(1):
                greet(near_sem, mem=peer)
        send_pair(i)
        if i == 2:
            pl.semaphore_wait(near_sem, 2)
            for peer in around(2):
                greet(far_sem, mem=peer)
    mid = (carry_l + carry_r).astype(BF16)
    spread[8] = mid[:, :128]
    spread[9] = mid[:, 128:]
    send_pair(steps)
    sub[15] = mid[:, :128]
    sub[16] = mid[:, 128:]

    def conv_pair(d):
        blocks = (8 - d, 7 + d)
        picked = jnp.concatenate([sub[nb_s[n, b]] for b in blocks for n in range(NB)], axis=1)
        none = jnp.zeros((NB * BLOCK, BLOCK), BF16)
        weights = jnp.concatenate(
            [
                jnp.concatenate([tiles_v[blocks[0]], none], axis=1),
                jnp.concatenate([none, tiles_v[blocks[1]]], axis=1),
            ],
            axis=0,
        )
        value = jnp.dot(picked, weights, preferred_element_type=F32).astype(BF16)
        smooth[1 + blocks[0]] = value[:, :BLOCK]
        smooth[1 + blocks[1]] = value[:, BLOCK:]

    def z_copy(owner, lanes):
        return pltpu.make_async_remote_copy(
            src_ref=part.at[owner, :, lanes],
            dst_ref=zrecv.at[z, :, lanes],
            send_sem=out_sem.at[2],
            recv_sem=out_sem.at[3],
            device_id={"mem": owner},
            device_id_type=MESH,
        )

    def interp(cb):
        i, h = cb // 2, cb % 2
        table = table_l.at[i] if i < steps else table_r.at[2 * steps - 1 - i]
        window = jnp.concatenate([smooth[cb], smooth[cb + 1], smooth[cb + 2]], axis=1)
        weights = table[h * BLOCK : h * BLOCK + 384, h * CB : (h + 1) * CB]
        back = jnp.dot(window, weights, preferred_element_type=F32)
        prod = back * anom_v[:, cb * CB : (cb + 1) * CB].astype(F32)
        part[i, :, h * CB : (h + 1) * CB] = jnp.sum(prod.reshape(8, 16, CB), axis=0).astype(BF16)

    def give(owner, lanes):
        @pl.when(owner != z)
        def _():
            z_copy(owner, lanes).start()

    def interp_step(i):
        for owner in (i, 2 * steps - 1 - i):
            interp(2 * owner)
            interp(2 * owner + 1)
            give(owner, slice(0, CP))

    def interp_half(inner):
        for owner in (0, 2 * steps - 1):
            h = int((owner == 0) == inner)
            interp(2 * owner + h)
            give(owner, slice(h * CB, (h + 1) * CB))

    for c in third:
        c.wait()

    def halo(i):
        for side, copy, recv, at, edge in (
            (has_left, to_right, lambda d: recv_l[8 - d], lambda d: 8 - d, lambda d: spread[1 - d]),
            (has_right, to_left, lambda d: recv_r[d], lambda d: 23 + d, lambda d: spread[16 + d]),
        ):
            span = range(2 * i, 2 * i + size(i))

            @pl.when(side)
            def _():
                copy(i).wait_recv()
                for d in span:
                    if d < 2:
                        sub[at(d)] = (edge(d).astype(F32) + recv(d).astype(F32)).astype(BF16)
                    else:
                        sub[at(d)] = recv(d)

            @pl.when(jnp.logical_not(side))
            def _():
                for d in span:
                    sub[at(d)] = edge(d) if d == 0 else jnp.zeros((128, 128), BF16)

    halo(0)
    conv_pair(1)
    for i in range(1, steps):
        halo(i)
        conv_pair(2 * i)
        conv_pair(2 * i + 1)
    pl.semaphore_wait(far_sem, 2)
    for s in range(EARLY):
        interp_step(steps - 1 - s)
    halo(steps)
    conv_pair(2 * steps)

    smooth_left = pltpu.make_async_remote_copy(
        src_ref=smooth.at[1],
        dst_ref=smooth.at[17],
        send_sem=out_sem.at[0],
        recv_sem=smooth_sem.at[0],
        device_id={"space": left},
        device_id_type=MESH,
    )
    smooth_right = pltpu.make_async_remote_copy(
        src_ref=smooth.at[16],
        dst_ref=smooth.at[0],
        send_sem=out_sem.at[1],
        recv_sem=smooth_sem.at[1],
        device_id={"space": right},
        device_id_type=MESH,
    )

    @pl.when(has_left)
    def _():
        smooth_left.start()

    @pl.when(has_right)
    def _():
        smooth_right.start()

    for s in range(EARLY, steps - 1):
        interp_step(steps - 1 - s)
    interp_half(True)

    @pl.when(has_left)
    def _():
        smooth_right.wait_recv()

    @pl.when(has_right)
    def _():
        smooth_left.wait_recv()

    @pl.when(jnp.logical_not(has_left))
    def _():
        smooth[0] = jnp.zeros((128, 128), BF16)

    @pl.when(jnp.logical_not(has_right))
    def _():
        smooth[17] = jnp.zeros((128, 128), BF16)

    interp_half(False)

    def sent(blocks, sem, **peer):
        return pltpu.make_async_remote_copy(
            src_ref=blocks,
            dst_ref=blocks,
            send_sem=out_sem.at[sem],
            recv_sem=out_sem.at[3],
            device_id=peer,
            device_id_type=MESH,
        )

    @pl.when(has_left)
    def _():
        sent(spread.at[0:10], 0, space=left).wait_send()

    @pl.when(has_right)
    def _():
        sent(spread.at[0:10], 1, space=right).wait_send()

    others = sent(zrecv.at[0 : 2 * steps - 1], 2, mem=lax.rem(z + 1, n_mem))
    others.wait_send()
    others.wait_recv()
    total = part[z].astype(F32)
    for off in range(1, n_mem):
        total = total + zrecv[lax.rem(z + off, n_mem)].astype(F32)
    out_ref[...] = total


def shards(increment, anomalies, interp_index, interp_weight, neighbour_blocks, tiles):
    n_space, n_mem = lax.axis_size("space"), lax.axis_size("mem")
    anomalies = anomalies.reshape(128, NCB * CB)
    tiles = tiles.reshape(16, NB * BLOCK, BLOCK)
    hbm = pl.BlockSpec(memory_space=pl.ANY)
    vmem = pltpu.VMEM
    dma = pltpu.SemaphoreType.DMA
    summed = pl.pallas_call(
        lambda *refs: kernel(n_space, n_mem, *refs),
        out_shape=pltpu.VMEM((16, CP), F32),
        in_specs=[hbm] * 6,
        out_specs=pl.BlockSpec(memory_space=pltpu.VMEM),
        scratch_shapes=[
            vmem((16, NCB * CB), F32),
            vmem((128, NCB * CB), BF16),
            vmem((INTP, NCB * CB), jnp.int32),
            vmem((INTP, NCB * CB), F32),
            pltpu.SMEM((NB, 16), jnp.int32),
            vmem((16, NB * BLOCK, BLOCK), BF16),
            vmem((4, WIN, CP), BF16),
            vmem((4, WIN, CP), BF16),
            vmem((18, 128, 128), BF16),
            vmem((9, 128, 128), BF16),
            vmem((9, 128, 128), BF16),
            vmem((32, 128, 128), BF16),
            vmem((18, 128, 128), BF16),
            vmem((8, 16, CP), BF16),
            vmem((8, 16, CP), BF16),
            dma((8,)),
            dma((5,)),
            dma((5,)),
            dma((2,)),
            dma((4,)),
            pltpu.SemaphoreType.REGULAR,
            pltpu.SemaphoreType.REGULAR,
        ],
        compiler_params=pltpu.CompilerParams(
            collective_id=0, has_side_effects=True, vmem_limit_bytes=VMEM_LIMIT
        ),
        name="nicas",
    )(increment, anomalies, interp_index, interp_weight, neighbour_blocks, tiles)
    return summed / (8 * n_mem - 1)


def solution(mesh):
    in_specs = (
        P(None, "space"),
        P("mem", None, "space"),
        P(None, "space"),
        P(None, "space"),
        P(None, "space"),
        P("space", None, None, None),
    )
    out_specs = P(None, ("space", "mem"))
    return jax.shard_map(shards, mesh=mesh, in_specs=in_specs, out_specs=out_specs, check_vma=False)
```

time: 27.7 us -> 25.6 us (0.924)
  local copies, waits for them, and re-layouts: 1.47 us -> 0 us
  Pallas kernels: 26.1 us -> 24.8 us
  other arithmetic: 0 us -> 0.64 us
    unnamed x1 -> x0, local copies, waits for them, and re-layouts: 1.47 us -> none
    pallas_call x1, Pallas kernels: 26.1 us -> 24.8 us  [shards(): pl.pallas_call(lambda *refs: kernel(n_space, n_mem, *refs), out_shape=plt...]
    div x0 -> x1, other arithmetic: none -> 0.64 us  [shards(): return summed / (8 * n_mem - 1)]
where the time goes in v3:
time: 25.6 us; the launch traced here: 25.5 us
  Pallas kernels  24.8 us (97%)
  other arithmetic  0.64 us (2%)
    pallas_call x1, Pallas kernels, shards(): pl.pallas_call(lambda *refs: kernel(n_space, n_mem, *refs), out_shape=plt...  24.8 us
    div x1, other arithmetic, shards(): return summed / (8 * n_mem - 1)  0.64 us

profile of v3, /device:TPU:2, one launch (start us, length us, event | category | flops | bytes accessed | tf_op | source)
XLA Modules:
  0.0 25.5 jit_solution(12400389884681111278)
XLA Ops:
  0.0 24.8 %nicas.1 = f32[16,1024]{1,0:T(8,128)S(1)} custom-call(f32[16,8192]{1,0:T(8,128)} %refs_0_.1, bf16[128,8192]{1,0:T(8,128)(2,1)} %bitcast.3, s32[3,8192]{1,0:T(4,128)} %refs_2_.1, f32[3,8192]{1,0:T(4,128)} %refs_3_.1, s32[9,16]{1,0:T(8,128)} %refs_4_.1, bf16[16,1152,128]{2,1,0:T(8,128)(2,1)} %bitcast.2), custom_call_target="tpu_custom_call" | custom-call | tf_op jit(solution)/shard_map/nicas/pallas_call | solution.py:404
  24.8 0.6 %broadcast_multiply_fusion = f32[16,1024]{1,0:T(8,128)} fusion(f32[16,1024]{1,0:T(8,128)S(1)} %nicas.1), kind=kLoop, calls=%fused_computation | loop fusion | flops 16384 | bytes 131072 | tf_op jit(solution)/shard_map/div | solution.py:438

commit v4 on v3

--- a/solution.py
+++ b/solution.py
@@ -16,7 +16,6 @@
 WIN = 512
 BAND = 288
 FIRST = 2
-EARLY = 3
 VMEM_LIMIT = 67_043_328 - 190 * 1024
 F32 = jnp.float32
 BF16 = jnp.bfloat16
@@ -98,7 +97,6 @@
     recv_r_sem,
     smooth_sem,
     out_sem,
-    near_sem,
     far_sem,
 ):
     me = lax.axis_index("space")
@@ -131,8 +129,9 @@
     for c in (*first, second, *third):
         c.start()
 
-    for peer in around(1):
-        greet(barrier, mem=peer)
+    for step in (1, 2):
+        for peer in around(step):
+            greet(barrier, mem=peer)
 
     @pl.when(has_left)
     def _():
@@ -218,14 +217,10 @@
                 sub[7 + 2 * i + h] = done_l[:, lanes]
                 sub[23 - 2 * i + h] = done_r[:, lanes]
         if i == 0:
-            pl.semaphore_wait(barrier, 2 + has_left.astype(jnp.int32) + has_right.astype(jnp.int32))
-            for peer in around(1):
-                greet(near_sem, mem=peer)
-        send_pair(i)
-        if i == 2:
-            pl.semaphore_wait(near_sem, 2)
+            pl.semaphore_wait(barrier, 4 + has_left.astype(jnp.int32) + has_right.astype(jnp.int32))
             for peer in around(2):
                 greet(far_sem, mem=peer)
+        send_pair(i)
     mid = (carry_l + carry_r).astype(BF16)
     spread[8] = mid[:, :128]
     spread[9] = mid[:, 128:]
@@ -276,6 +271,9 @@
         for owner in (i, 2 * steps - 1 - i):
             interp(2 * owner)
             interp(2 * owner + 1)
+
+    def give_step(i):
+        for owner in (i, 2 * steps - 1 - i):
             give(owner, slice(0, CP))
 
     def interp_half(inner):
@@ -310,13 +308,16 @@
 
     halo(0)
     conv_pair(1)
-    for i in range(1, steps):
+    for i in range(1, steps - 1):
         halo(i)
         conv_pair(2 * i)
         conv_pair(2 * i + 1)
+    interp_step(3)
+    interp_step(2)
     pl.semaphore_wait(far_sem, 2)
-    for s in range(EARLY):
-        interp_step(steps - 1 - s)
+    give_step(3)
+    give_step(2)
+    halo(steps - 1)
     halo(steps)
     conv_pair(2 * steps)
 
@@ -345,8 +346,10 @@
     def _():
         smooth_right.start()
 
-    for s in range(EARLY, steps - 1):
-        interp_step(steps - 1 - s)
+    conv_pair(2 * steps - 2)
+    conv_pair(2 * steps - 1)
+    interp_step(1)
+    give_step(1)
     interp_half(True)
 
     @pl.when(has_left)
@@ -428,7 +431,6 @@
             dma((2,)),
             dma((4,)),
             pltpu.SemaphoreType.REGULAR,
-            pltpu.SemaphoreType.REGULAR,
         ],
         compiler_params=pltpu.CompilerParams(
             collective_id=0, has_side_effects=True, vmem_limit_bytes=VMEM_LIMIT

time: 25.6 us -> 24.2 us (0.945)
  Pallas kernels: 24.8 us -> 23.4 us
    pallas_call x1, Pallas kernels: 24.8 us -> 23.4 us  [shards(): pl.pallas_call(lambda *refs: kernel(n_space, n_mem, *refs), out_shape=plt...]
where the time goes in v4:
time: 24.2 us; the launch traced here: 24.1 us
  Pallas kernels  23.4 us (97%)
  other arithmetic  0.64 us (3%)
    pallas_call x1, Pallas kernels, shards(): pl.pallas_call(lambda *refs: kernel(n_space, n_mem, *refs), out_shape=plt...  23.4 us
    div x1, other arithmetic, shards(): return summed / (8 * n_mem - 1)  0.64 us

profile of v4, /device:TPU:2, one launch (start us, length us, event | category | flops | bytes accessed | tf_op | source)
XLA Modules:
  0.0 24.1 jit_solution(14768157500736607425)
XLA Ops:
  0.0 23.4 %nicas.1 = f32[16,1024]{1,0:T(8,128)S(1)} custom-call(f32[16,8192]{1,0:T(8,128)} %refs_0_.1, bf16[128,8192]{1,0:T(8,128)(2,1)} %bitcast.3, s32[3,8192]{1,0:T(4,128)} %refs_2_.1, f32[3,8192]{1,0:T(4,128)} %refs_3_.1, s32[9,16]{1,0:T(8,128)} %refs_4_.1, bf16[16,1152,128]{2,1,0:T(8,128)(2,1)} %bitcast.2), custom_call_target="tpu_custom_call" | custom-call | tf_op jit(solution)/shard_map/nicas/pallas_call | solution.py:407
  23.4 0.6 %broadcast_multiply_fusion = f32[16,1024]{1,0:T(8,128)} fusion(f32[16,1024]{1,0:T(8,128)S(1)} %nicas.1), kind=kLoop, calls=%fused_computation | loop fusion | flops 16384 | bytes 131072 | tf_op jit(solution)/shard_map/div | solution.py:440

commit v5 on v4

--- a/solution.py
+++ b/solution.py
@@ -97,7 +97,6 @@
     recv_r_sem,
     smooth_sem,
     out_sem,
-    far_sem,
 ):
     me = lax.axis_index("space")
     z = lax.axis_index("mem")
@@ -110,28 +109,31 @@
     def greet(sem, **peer):
         pl.semaphore_signal(sem, inc=1, device_id=peer, device_id_type=MESH)
 
-    def around(step):
-        return lax.rem(z + step, n_mem), lax.rem(z + n_mem - step, n_mem)
-
-    lo, hi = FIRST * CB, (NCB - FIRST) * CB
-    first = [
+    def columns(src, dst, low, high, sem):
+        cols = slice(low * CB, high * CB)
+        return pltpu.make_async_copy(src.at[:, cols], dst.at[:, cols], in_sem.at[sem])
+
+    def fields(low, high, sem):
+        return [
+            columns(inc_h, inc_v, low, high, sem),
+            columns(anom_h, anom_v, low, high, sem + 1),
+        ]
+
+    where = [
         pltpu.make_async_copy(idx_h, idx_v, in_sem.at[0]),
         pltpu.make_async_copy(wgt_h, wgt_v, in_sem.at[1]),
-        pltpu.make_async_copy(inc_h, inc_v, in_sem.at[2]),
-        pltpu.make_async_copy(anom_h.at[:, :lo], anom_v.at[:, :lo], in_sem.at[3]),
-        pltpu.make_async_copy(anom_h.at[:, hi:], anom_v.at[:, hi:], in_sem.at[4]),
     ]
-    second = pltpu.make_async_copy(anom_h.at[:, lo:hi], anom_v.at[:, lo:hi], in_sem.at[5])
+    first_l, first_r = fields(0, FIRST, 2), fields(NCB - FIRST, NCB, 4)
+    second = fields(FIRST, NCB - FIRST, 6)
     third = [
-        pltpu.make_async_copy(nb_h, nb_s, in_sem.at[6]),
-        pltpu.make_async_copy(tiles_h, tiles_v, in_sem.at[7]),
+        pltpu.make_async_copy(nb_h, nb_s, in_sem.at[8]),
+        pltpu.make_async_copy(tiles_h, tiles_v, in_sem.at[9]),
     ]
-    for c in (*first, second, *third):
+    for c in (*where, *first_l, *first_r, *second, *third):
         c.start()
 
-    for step in (1, 2):
-        for peer in around(step):
-            greet(barrier, mem=peer)
+    for step in range(1, n_mem):
+        greet(barrier, mem=lax.rem(z + step, n_mem))
 
     @pl.when(has_left)
     def _():
@@ -194,7 +196,7 @@
             for h in range(2)
         ]
 
-    for c in first:
+    for c in (*where, *first_l, *first_r):
         c.wait()
     carry_l = carry_r = None
 
@@ -203,7 +205,8 @@
 
     for i in range(steps):
         if i == FIRST // 2:
-            second.wait()
+            for c in second:
+                c.wait()
         win_l = spread_window(2 * i, table_l.at[i])
         win_r = spread_window(NCB - 2 - 2 * i, table_r.at[i])
         done_l = plus(win_l[0], carry_l).astype(BF16)
@@ -217,9 +220,8 @@
                 sub[7 + 2 * i + h] = done_l[:, lanes]
                 sub[23 - 2 * i + h] = done_r[:, lanes]
         if i == 0:
-            pl.semaphore_wait(barrier, 4 + has_left.astype(jnp.int32) + has_right.astype(jnp.int32))
-            for peer in around(2):
-                greet(far_sem, mem=peer)
+            peers = n_mem - 1 + has_left.astype(jnp.int32) + has_right.astype(jnp.int32)
+            pl.semaphore_wait(barrier, peers)
         send_pair(i)
     mid = (carry_l + carry_r).astype(BF16)
     spread[8] = mid[:, :128]
@@ -267,14 +269,9 @@
         def _():
             z_copy(owner, lanes).start()
 
-    def interp_step(i):
-        for owner in (i, 2 * steps - 1 - i):
-            interp(2 * owner)
-            interp(2 * owner + 1)
-
-    def give_step(i):
-        for owner in (i, 2 * steps - 1 - i):
-            give(owner, slice(0, CP))
+    def interp_owner(owner):
+        interp(2 * owner)
+        interp(2 * owner + 1)
 
     def interp_half(inner):
         for owner in (0, 2 * steps - 1):
@@ -312,11 +309,11 @@
         halo(i)
         conv_pair(2 * i)
         conv_pair(2 * i + 1)
-    interp_step(3)
-    interp_step(2)
-    pl.semaphore_wait(far_sem, 2)
-    give_step(3)
-    give_step(2)
+    inner = (steps - 1, steps, steps - 2, steps + 1)
+    for owner in inner:
+        interp_owner(owner)
+    for owner in inner:
+        give(owner, slice(0, CP))
     halo(steps - 1)
     halo(steps)
     conv_pair(2 * steps)
@@ -348,9 +345,10 @@
 
     conv_pair(2 * steps - 2)
     conv_pair(2 * steps - 1)
-    interp_step(1)
-    give_step(1)
     interp_half(True)
+    for owner in (1, 2 * steps - 2):
+        interp_owner(owner)
+        give(owner, slice(0, CP))
 
     @pl.when(has_left)
     def _():
@@ -425,12 +423,11 @@
             vmem((18, 128, 128), BF16),
             vmem((8, 16, CP), BF16),
             vmem((8, 16, CP), BF16),
-            dma((8,)),
+            dma((10,)),
             dma((5,)),
             dma((5,)),
             dma((2,)),
             dma((4,)),
-            pltpu.SemaphoreType.REGULAR,
         ],
         compiler_params=pltpu.CompilerParams(
             collective_id=0, has_side_effects=True, vmem_limit_bytes=VMEM_LIMIT

time: 24.2 us -> 24 us (level)
  no operation moved by 1% of the time
where the time goes in v5:
time: 24 us; the launch traced here: 23.9 us
  Pallas kernels  23.3 us (97%)
  other arithmetic  0.64 us (3%)
    pallas_call x1, Pallas kernels, shards(): pl.pallas_call(lambda *refs: kernel(n_space, n_mem, *refs), out_shape=plt...  23.3 us
    div x1, other arithmetic, shards(): return summed / (8 * n_mem - 1)  0.64 us

profile of v5, /device:TPU:2, one launch (start us, length us, event | category | flops | bytes accessed | tf_op | source)
XLA Modules:
  0.0 23.9 jit_solution(15501214026063471488)
XLA Ops:
  0.0 23.3 %nicas.1 = f32[16,1024]{1,0:T(8,128)S(1)} custom-call(f32[16,8192]{1,0:T(8,128)} %refs_0_.1, bf16[128,8192]{1,0:T(8,128)(2,1)} %bitcast.3, s32[3,8192]{1,0:T(4,128)} %refs_2_.1, f32[3,8192]{1,0:T(4,128)} %refs_3_.1, s32[9,16]{1,0:T(8,128)} %refs_4_.1, bf16[16,1152,128]{2,1,0:T(8,128)(2,1)} %bitcast.2), custom_call_target="tpu_custom_call" | custom-call | tf_op jit(solution)/shard_map/nicas/pallas_call | solution.py:405
  23.3 0.6 %broadcast_multiply_fusion = f32[16,1024]{1,0:T(8,128)} fusion(f32[16,1024]{1,0:T(8,128)S(1)} %nicas.1), kind=kLoop, calls=%fused_computation | loop fusion | flops 16384 | bytes 131072 | tf_op jit(solution)/shard_map/div | solution.py:437
